TPU v7x, 32 devices: a whole 2x2x4 slice. The times are simulated.
32 devices in a mesh: rep: 2 (over x), exp: 16 (over z, y, core).
Axes of the slice: x: 2, y: 2, z: 4, core: 2. Of those that a mesh axis runs over, the one named last changes fastest.
Arguments:
- tokens: bfloat16 [1, 128, 7168], P(None, 'exp', 'rep'), may hold values from -6 to 6
- gate_up: bfloat16 [16, 7168, 2, 2048], P('exp', 'rep'), may hold values from -0.09375 to 0.09375
- w_down: bfloat16 [16, 2048, 7168], P('exp', None, 'rep'), may hold values from -0.125 to 0.125
- routes: int32 [1, 128, 8], P(None, 'exp'), may hold values from 0 to 15, all different within a row; in each aligned block of 8 rows (0 to 7, 8 to 15, ..., all dimensions but the last counted through in order) at most 8 rows name the same one
- gates: float32 [1, 128, 8], P(None, 'exp'), may hold values from 0.05 to 1
Outputs:
- mixed_out: bfloat16 [1, 128, 7168], P(None, 'exp', 'rep')
Inputs may be any that keep to these rules, and one draw needn't show every extreme that they name: `routes`: within one step, the 8 tokens of one index of exp name any expert at most 8 times, a bound that some block reaches.
All inputs are finite; a program needn't handle non-finite values.
Results may differ from a plain program's by a relative error of at most 0.024.
Values may be sent and summed in bfloat16 or wider, within the bound.
A program may use at most 192 MiB of HBM per device.

v0:
```python
import functools

import jax
import jax.numpy as jnp
from jax import lax
from jax.experimental import pallas as pl
from jax.experimental.pallas import tpu as pltpu
from jax.sharding import PartitionSpec as P


def silu_glu(summed):
    return (jax.nn.silu(summed[:, 0]) * summed[:, 1]).astype(jnp.bfloat16)


def on_device(tokens, gate_up, w_down, routes, gates):
    steps_all, local_tokens, slab_width = tokens.shape
    top_count = routes.shape[2]
    groups = lax.axis_size("exp")
    experts = gate_up.shape[0] * groups
    capacity = max(2, 2 * local_tokens * top_count // experts)
    hidden_units = w_down.shape[1]
    row_count = groups * capacity
    weights_in = gate_up[0].reshape(slab_width, 2 * hidden_units)
    weights_out = w_down[0]
    labels = jnp.arange(experts * capacity, dtype=jnp.int32)
    expert_range = jnp.arange(experts, dtype=jnp.int32)
    expert_ids = routes[0].reshape(-1)
    onehot = (expert_ids[:, None] == expert_range[None, :]).astype(jnp.int32)
    before = jnp.cumsum(onehot, axis=0) - onehot
    slot_rank = jnp.sum(before * onehot, axis=1)
    target_row = expert_ids * capacity + slot_rank
    target_grid = target_row.reshape(local_tokens, top_count)
    placing = jnp.sum(
        (labels[:, None, None] == target_grid[None, :, :]).astype(jnp.int32), axis=2
    ).astype(jnp.bfloat16)
    outgoing = jnp.dot(placing, tokens[0], preferred_element_type=jnp.float32).astype(jnp.bfloat16)
    outgoing = outgoing.reshape(experts, capacity, slab_width)
    arrived = lax.all_to_all(outgoing, "exp", split_axis=0, concat_axis=0, tiled=True)
    partial_value = jnp.dot(
        arrived.reshape(row_count, slab_width), weights_in, preferred_element_type=jnp.float32
    )
    partial_value = partial_value.reshape(row_count, 2, hidden_units)
    shares = lax.psum_scatter(
        partial_value.astype(jnp.bfloat16), "rep", scatter_dimension=0, tiled=True
    ).astype(jnp.float32)
    hidden = silu_glu(shares)
    produced = jnp.dot(
        lax.all_gather(hidden, "rep", axis=0, tiled=True),
        weights_out,
        preferred_element_type=jnp.float32,
    )
    expert_out = produced.astype(jnp.bfloat16).reshape(groups, capacity, slab_width)
    returned = lax.all_to_all(expert_out, "exp", split_axis=0, concat_axis=0, tiled=True).reshape(
        experts * capacity, slab_width
    )
    picked = returned[target_row].reshape(local_tokens, top_count, slab_width).astype(jnp.float32)
    mixed_out = jnp.sum(gates[0][:, :, None] * picked, axis=1).astype(jnp.bfloat16)
    outputs = [mixed_out]
    return jnp.stack(outputs)


def fused_kernel(
    n, chunks, pieces, tok_ref, gu_ref, dn_ref, routes_ref, gates_ref, out_ref,
    xg, wgu, wdn, x2, pbuf, prec, hid, hfull, cbuf, crec, ybuf, yrec, zbuf, zrec,
    gu_sem, dn_sem, dz_s, dz_r, dy_s, dy_r, dc_s, dc_r,
    ps_s, ps_r, hs_s, hs_r, rc_s, rc_r, ry_s, ry_r, rz_s, rz_r,
):
    rep = lax.axis_index("rep")
    me = lax.axis_index("exp")
    zs = n // 4
    c, y, z = lax.rem(me, 2), lax.rem(me // 2, 2), me // 4
    rows, width = tok_ref.shape
    hidden_units = dn_ref.shape[0]
    cw, pw = hidden_units // chunks, width // pieces
    half = n * rows // 2
    other = 1 - rep
    core_peer = z * 4 + y * 2 + (1 - c)
    y_peer = z * 4 + (1 - y) * 2 + c

    def z_peer(d):
        return lax.rem(z + d, zs) * 4 + y * 2 + c

    def remote(src, dst, send, recv, to):
        return pltpu.make_async_remote_copy(
            src_ref=src, dst_ref=dst, send_sem=send, recv_sem=recv,
            device_id=to, device_id_type=pl.DeviceIdType.MESH,
        )

    barrier = pltpu.get_barrier_semaphore()
    peers = [(other, me), (rep, core_peer), (rep, y_peer)] + [(rep, z_peer(d)) for d in range(1, zs)]
    for peer in peers:
        pl.semaphore_signal(barrier, inc=1, device_id=peer, device_id_type=pl.DeviceIdType.MESH)

    def gu_copy(j):
        return pltpu.make_async_copy(
            gu_ref.at[:, :, pl.ds(pl.multiple_of(j * cw, 128), cw)], wgu.at[j], gu_sem.at[j]
        )

    def dn_copy(q):
        cols = pl.ds(q * pw, pw)
        return pltpu.make_async_copy(dn_ref.at[:, cols], wdn.at[:, cols], dn_sem.at[q])

    for j in range(chunks):
        gu_copy(j).start()
    for q in range(pieces):
        dn_copy(q).start()

    lane = lax.broadcasted_iota(jnp.int32, (rows, 128), 1)
    weight = jnp.zeros((rows, 128), jnp.float32)
    for k in range(routes_ref.shape[1]):
        hit = routes_ref[:, k : k + 1] == lax.rem(lane, n)
        weight = weight + jnp.where(hit, gates_ref[:, k : k + 1], 0.0)
    high = weight.astype(jnp.bfloat16).astype(jnp.float32)
    packed = jnp.where(lane < n, high, jnp.where(lane < 2 * n, weight - high, 0.0))
    xg[me, :, 0:width] = tok_ref[...]
    xg[me, :, width : width + 128] = packed.astype(jnp.bfloat16)
    pl.semaphore_wait(barrier, len(peers))

    def source(d, yy):
        return lax.rem(z - d + zs, zs) * 4 + yy * 2 + c

    def to_z(d):
        return remote(xg.at[me], xg.at[me], dz_s.at[d], dz_r.at[d], (rep, z_peer(d)))

    def to_y(d):
        slot = xg.at[source(d, y)]
        return remote(slot, slot, dy_s.at[d], dy_r.at[d], (rep, y_peer))

    def to_c(d, far):
        slot = xg.at[source(d, 1 - y if far else y)]
        at = d + zs * far
        return remote(slot, slot, dc_s.at[at], dc_r.at[at], (rep, core_peer))

    for d in range(1, zs):
        to_z(d).start()
    to_y(0).start()
    to_c(0, 0).start()
    for d in range(1, zs):
        to_z(d).wait_recv()
        to_y(d).start()
        to_c(d, 0).start()
    for d in range(zs):
        to_y(d).wait_recv()
        to_c(d, 1).start()
    for far in range(2):
        for d in range(zs):
            to_c(d, far).wait_recv()

    row_at = lax.broadcasted_iota(jnp.int32, (128, 512), 0)
    col_at = lax.broadcasted_iota(jnp.int32, (128, 512), 1)
    target = jnp.where(col_at < 256, 2 * row_at, 256 + 2 * row_at + 1)
    spread = jnp.where(col_at == target, 1.0, 0.0).astype(jnp.bfloat16)

    @pl.loop(0, width // 128, unroll=14)
    def _(b):
        part = xg[:, :, pl.ds(pl.multiple_of(b * 128, 128), 128)].reshape(2 * half, 128)
        both = jnp.dot(part, spread, preferred_element_type=jnp.float32).astype(jnp.bfloat16)
        cols = pl.ds(pl.multiple_of(b * 256, 256), 256)
        for h in range(2):
            x2[2 * h * half : (2 * h + 1) * half, cols] = both[h * half : (h + 1) * half, :256]
            x2[(2 * h + 1) * half : (2 * h + 2) * half, cols] = both[h * half : (h + 1) * half, 256:]

    def partial_send(j):
        return remote(pbuf.at[j, other], prec.at[j], ps_s.at[j], ps_r.at[j], (other, me))

    def hidden_send(j):
        return remote(hid.at[j, rep], hid.at[j, rep], hs_s.at[j], hs_r.at[j], (other, me))

    def hidden_recv(j):
        return remote(hid.at[j, other], hid.at[j, other], hs_s.at[j], hs_r.at[j], (other, me))

    def finish(j):
        partial_send(j).wait_recv()
        total = pbuf[j, rep].astype(jnp.float32) + prec[j].astype(jnp.float32)
        hid[j, rep] = (jax.nn.silu(total[:half]) * total[half:]).astype(jnp.bfloat16)
        hidden_send(j).start()

    lag = 2

    @pl.loop(0, chunks)
    def _(j):
        gu_copy(j).wait()
        weights = wgu[j].reshape(2 * width, cw)
        acc = jnp.dot(x2[...], weights, preferred_element_type=jnp.float32)
        pbuf[j] = acc.astype(jnp.bfloat16).reshape(2, 2 * half, cw)
        partial_send(j).start()

        @pl.when(j >= lag)
        def _():
            finish(j - lag)

    for j in range(chunks - lag, chunks):
        finish(j)
    for j in range(chunks):
        hidden_recv(j).wait_recv()
        hfull[:, j * cw : (j + 1) * cw] = hid[j].reshape(2 * half, cw)

    mark = lax.broadcasted_iota(jnp.int32, (2 * half, 128), 1)
    pair = xg[:, :, width : width + 128].reshape(2 * half, 128).astype(jnp.float32)
    scale = jnp.sum(jnp.where(lax.rem(mark, n) == me, pair, 0.0), axis=1, keepdims=True)

    def core_send(q):
        return remote(cbuf.at[q, 1 - c], crec.at[q], rc_s.at[q], rc_r.at[q], (rep, core_peer))

    def y_send(q):
        return remote(ybuf.at[q, 1 - y], yrec.at[q], ry_s.at[q], ry_r.at[q], (rep, y_peer))

    def z_send(q, d):
        return remote(
            zbuf.at[q, lax.rem(z + d, zs)], zrec.at[q, d], rz_s.at[q, d], rz_r.at[q, d], (rep, z_peer(d))
        )

    def produce(q):
        dn_copy(q).wait()
        made = jnp.dot(hfull[...], wdn[:, q * pw : (q + 1) * pw], preferred_element_type=jnp.float32)
        mixed = (made.astype(jnp.bfloat16).astype(jnp.float32) * scale).astype(jnp.bfloat16)
        mixed = mixed.reshape(n, rows, pw)
        for g in range(n):
            cbuf[q, g % 2, (g // 2) % 2, g // 4] = mixed[g]
        core_send(q).start()

    def over_core(q):
        core_send(q).wait_recv()
        ybuf[q] = (cbuf[q, c].astype(jnp.float32) + crec[q].astype(jnp.float32)).astype(jnp.bfloat16)
        y_send(q).start()

    def over_y(q):
        y_send(q).wait_recv()
        zbuf[q] = (ybuf[q, y].astype(jnp.float32) + yrec[q].astype(jnp.float32)).astype(jnp.bfloat16)
        for d in range(1, zs):
            z_send(q, d).start()

    def over_z(q):
        total = zbuf[q, z].astype(jnp.float32)
        for d in range(1, zs):
            z_send(q, d).wait_recv()
            total = total + zrec[q, d].astype(jnp.float32)
        out_ref[:, q * pw : (q + 1) * pw] = total.astype(jnp.bfloat16)

    for step in range(pieces + 3):
        for late, stage in enumerate((produce, over_core, over_y, over_z)):
            if 0 <= step - late < pieces:
                stage(step - late)

    for d in range(1, zs):
        to_z(d).wait_send()
    for d in range(zs):
        to_y(d).wait_send()
        for far in range(2):
            to_c(d, far).wait_send()
    for j in range(chunks):
        partial_send(j).wait_send()
        hidden_send(j).wait_send()
    for q in range(pieces):
        core_send(q).wait_send()
        y_send(q).wait_send()
        for d in range(1, zs):
            z_send(q, d).wait_send()


def fused_on_device(tokens, gate_up, w_down, routes, gates):
    n = lax.axis_size("exp")
    _, rows, width = tokens.shape
    hidden_units = w_down.shape[1]
    chunks, pieces = hidden_units // 256, 2
    pw, zs, half = width // pieces, n // 4, n * rows // 2
    bf16, dma = jnp.bfloat16, pltpu.SemaphoreType.DMA
    vmem = pl.BlockSpec(memory_space=pltpu.VMEM)
    anywhere = pl.BlockSpec(memory_space=pl.ANY)
    mixed_out = pl.pallas_call(
        functools.partial(fused_kernel, n, chunks, pieces),
        out_shape=jax.ShapeDtypeStruct((rows, width), bf16),
        in_specs=[vmem, anywhere, anywhere, vmem, vmem],
        out_specs=vmem,
        scratch_shapes=[
            pltpu.VMEM((n, rows, width + 128), bf16),
            pltpu.VMEM((chunks, width, 2, 256), bf16),
            pltpu.VMEM((hidden_units, width), bf16),
            pltpu.VMEM((4 * half, 2 * width), bf16),
            pltpu.VMEM((chunks, 2, 2 * half, 256), bf16),
            pltpu.VMEM((chunks, 2 * half, 256), bf16),
            pltpu.VMEM((chunks, 2, half, 256), bf16),
            pltpu.VMEM((2 * half, hidden_units), bf16),
            pltpu.VMEM((pieces, 2, 2, zs, rows, pw), bf16),
            pltpu.VMEM((pieces, 2, zs, rows, pw), bf16),
            pltpu.VMEM((pieces, 2, zs, rows, pw), bf16),
            pltpu.VMEM((pieces, zs, rows, pw), bf16),
            pltpu.VMEM((pieces, zs, rows, pw), bf16),
            pltpu.VMEM((pieces, zs, rows, pw), bf16),
            dma((chunks,)), dma((pieces,)),
            dma((zs,)), dma((zs,)), dma((zs,)), dma((zs,)), dma((2 * zs,)), dma((2 * zs,)),
            dma((chunks,)), dma((chunks,)), dma((chunks,)), dma((chunks,)),
            dma((pieces,)), dma((pieces,)), dma((pieces,)), dma((pieces,)),
            dma((pieces, zs)), dma((pieces, zs)),
        ],
        compiler_params=pltpu.CompilerParams(
            collective_id=0, has_side_effects=True, vmem_limit_bytes=67043328
        ),
    )(tokens[0], gate_up[0], w_down[0], routes[0], gates[0])
    return mixed_out[None]


def fits(mesh):
    return mesh.shape["rep"] == 2 and mesh.shape["exp"] % 4 == 0 and mesh.shape["exp"] <= 16


def solution(mesh):
    placed = (
        P(None, "exp", "rep"),
        P("exp", "rep", None, None),
        P("exp", None, "rep"),
        P(None, "exp", None),
        P(None, "exp", None),
    )
    return jax.shard_map(
        fused_on_device if fits(mesh) else on_device, mesh=mesh, in_specs=placed, out_specs=P(None, "exp", "rep"), check_vma=False
    )
```

profile of v0, /device:TPU:0, one launch (start us, length us, event | category | flops | bytes accessed | tf_op | source)
XLA Modules:
  0.0 56.1 jit_solution(11297135078151963458)
XLA Ops:
  0.0 54.7 %shard_map.55 = bf16[8,3584]{1,0:T(8,128)(2,1)} custom-call(bf16[8,3584]{1,0:T(8,128)(2,1)} %bitcast.9, bf16[3584,2,2048]{2,1,0:T(2,128)(2,1)} %bitcast.6, bf16[2048,3584]{1,0:T(8,128)(2,1)} %bitcast.7, s32[8,8]{1,0:T(8,128)} %bitcast.10, f32[8,8]{1,0:T(8,128)} %bitcast.11), custom_call_target="tpu_custom_call" | custom-call | tf_op jit(solution)/shard_map/pallas_call | solution.py:270
  54.7 1.4 %copy.7 = bf16[1,8,3584]{2,1,0:T(8,128)(2,1)} copy(bf16[1,8,3584]{2,1,0:T(8,128)(2,1)} %bitcast.8) | data formatting | bytes 114688
where the time goes:
time: 56.3 us; the launch traced here: 56.1 us
  Pallas kernels  54.7 us (97%)
  local copies, waits for them, and re-layouts  1.45 us (3%)
    pallas_call x1, Pallas kernels, fused_on_device(): pl.pallas_call(functools.partial(fused_kernel, n, chunks, pieces), out_sh...  54.7 us
    unnamed x1, local copies, waits for them, and re-layouts  1.45 us

commit v1 on v0

v1 whole, which is shorter than its diff:
```python
import functools

import jax
import jax.numpy as jnp
from jax import lax
from jax.experimental import pallas as pl
from jax.experimental.pallas import tpu as pltpu
from jax.sharding import PartitionSpec as P


def silu_glu(summed):
    return (jax.nn.silu(summed[:, 0]) * summed[:, 1]).astype(jnp.bfloat16)


def on_device(tokens, gate_up, w_down, routes, gates):
    steps_all, local_tokens, slab_width = tokens.shape
    top_count = routes.shape[2]
    groups = lax.axis_size("exp")
    experts = gate_up.shape[0] * groups
    capacity = max(2, 2 * local_tokens * top_count // experts)
    hidden_units = w_down.shape[1]
    row_count = groups * capacity
    weights_in = gate_up[0].reshape(slab_width, 2 * hidden_units)
    weights_out = w_down[0]
    labels = jnp.arange(experts * capacity, dtype=jnp.int32)
    expert_range = jnp.arange(experts, dtype=jnp.int32)
    expert_ids = routes[0].reshape(-1)
    onehot = (expert_ids[:, None] == expert_range[None, :]).astype(jnp.int32)
    before = jnp.cumsum(onehot, axis=0) - onehot
    slot_rank = jnp.sum(before * onehot, axis=1)
    target_row = expert_ids * capacity + slot_rank
    target_grid = target_row.reshape(local_tokens, top_count)
    placing = jnp.sum(
        (labels[:, None, None] == target_grid[None, :, :]).astype(jnp.int32), axis=2
    ).astype(jnp.bfloat16)
    outgoing = jnp.dot(placing, tokens[0], preferred_element_type=jnp.float32).astype(jnp.bfloat16)
    outgoing = outgoing.reshape(experts, capacity, slab_width)
    arrived = lax.all_to_all(outgoing, "exp", split_axis=0, concat_axis=0, tiled=True)
    partial_value = jnp.dot(
        arrived.reshape(row_count, slab_width), weights_in, preferred_element_type=jnp.float32
    )
    partial_value = partial_value.reshape(row_count, 2, hidden_units)
    shares = lax.psum_scatter(
        partial_value.astype(jnp.bfloat16), "rep", scatter_dimension=0, tiled=True
    ).astype(jnp.float32)
    hidden = silu_glu(shares)
    produced = jnp.dot(
        lax.all_gather(hidden, "rep", axis=0, tiled=True),
        weights_out,
        preferred_element_type=jnp.float32,
    )
    expert_out = produced.astype(jnp.bfloat16).reshape(groups, capacity, slab_width)
    returned = lax.all_to_all(expert_out, "exp", split_axis=0, concat_axis=0, tiled=True).reshape(
        experts * capacity, slab_width
    )
    picked = returned[target_row].reshape(local_tokens, top_count, slab_width).astype(jnp.float32)
    mixed_out = jnp.sum(gates[0][:, :, None] * picked, axis=1).astype(jnp.bfloat16)
    outputs = [mixed_out]
    return jnp.stack(outputs)


def fused_kernel(
    chunks, pieces, lag, tok_ref, gu_ref, dn_ref, routes_ref, gates_ref, out_ref,
    xg, wgu, wdn, x2, pbuf, prec, hid, dacc, cbuf, crec, rbuf, rrec, oacc, fbuf, frec,
    gu_sem, dn_sem, ag_s, ag_r, mi_s, mi_r, dc_s, dc_r,
    ps_s, ps_r, hs_s, hs_r, rc_s, rc_r, rr_s, rr_r, rf_s, rf_r,
):
    rep = lax.axis_index("rep")
    me = lax.axis_index("exp")
    c, y, zl, pair = lax.rem(me, 2), lax.rem(me // 2, 2), lax.rem(me // 4, 2), me // 8
    rows, width = tok_ref.shape
    hidden_units = dn_ref.shape[0]
    n = 16
    cw, pw = hidden_units // chunks, width // pieces
    group, half = 8 * rows, 4 * rows
    other = 1 - rep
    at = zl * 4 + y * 2 + c
    base = pair * 8
    x_peer = (other, me)
    core_peer = (rep, base + zl * 4 + y * 2 + 1 - c)
    far_peer = (rep, (1 - pair) * 8 + at)
    near = [
        (1 - zl, y),
        (1 - zl, 1 - y),
        (zl, 1 - y),
    ]
    near_peers = [(rep, base + a * 4 + b * 2 + c) for a, b in near]

    def remote(src, dst, send, recv, to):
        return pltpu.make_async_remote_copy(
            src_ref=src, dst_ref=dst, send_sem=send, recv_sem=recv,
            device_id=to, device_id_type=pl.DeviceIdType.MESH,
        )

    barrier = pltpu.get_barrier_semaphore()
    peers = [x_peer, core_peer, far_peer] + near_peers
    for peer in peers:
        pl.semaphore_signal(barrier, inc=1, device_id=peer, device_id_type=pl.DeviceIdType.MESH)

    gu_rows = gu_ref.reshape(2 * width, hidden_units)

    def gu_copy(j):
        return pltpu.make_async_copy(
            gu_rows.at[:, pl.ds(pl.multiple_of(j * cw, 128), cw)], wgu.at[j], gu_sem.at[j]
        )

    def dn_copy(q):
        cols = pl.ds(q * pw, pw)
        return pltpu.make_async_copy(dn_ref.at[:, cols], wdn.at[:, cols], dn_sem.at[q])

    for j in range(chunks):
        gu_copy(j).start()
    for q in range(pieces):
        dn_copy(q).start()

    lane = lax.broadcasted_iota(jnp.int32, (rows, 128), 1)
    weight = jnp.zeros((rows, 128), jnp.float32)
    for k in range(routes_ref.shape[1]):
        hit = routes_ref[:, k : k + 1] == lax.rem(lane, n)
        weight = weight + jnp.where(hit, gates_ref[:, k : k + 1], 0.0)
    high = weight.astype(jnp.bfloat16).astype(jnp.float32)
    packed = jnp.where(lane < n, high, jnp.where(lane < 2 * n, weight - high, 0.0))
    xg[0, at, :, 0:width] = tok_ref[...]
    xg[0, at, :, width : width + 128] = packed.astype(jnp.bfloat16)
    pl.semaphore_wait(barrier, len(peers))

    def gather(g, e):
        slot = xg.at[g, at]
        return remote(slot, slot, ag_s.at[g, e], ag_r.at[g, e], near_peers[e])

    def mirror():
        return remote(xg.at[0, at], xg.at[1, at], mi_s, mi_r, far_peer)

    def to_core(g, e):
        a, b = (near + [(zl, y)])[e]
        slot = xg.at[g, a * 4 + b * 2 + c]
        return remote(slot, slot, dc_s.at[g, e], dc_r.at[g, e], core_peer)

    def spread_group(g):
        row_at = lax.broadcasted_iota(jnp.int32, (128, 512), 0)
        col_at = lax.broadcasted_iota(jnp.int32, (128, 512), 1)
        target = jnp.where(col_at < 256, 2 * row_at, 256 + 2 * row_at + 1)
        spread = jnp.where(col_at == target, 1.0, 0.0).astype(jnp.bfloat16)
        batch = 7

        @pl.loop(0, width // (128 * batch))
        def _(t):
            parts = [
                xg[g, :, :, pl.ds(pl.multiple_of((t * batch + i) * 128, 128), 128)].reshape(group, 128)
                for i in range(batch)
            ]
            both = jnp.dot(
                jnp.concatenate(parts, axis=0), spread, preferred_element_type=jnp.float32
            ).astype(jnp.bfloat16)
            for i in range(batch):
                cols = pl.ds(pl.multiple_of((t * batch + i) * 256, 256), 256)
                for h in range(2):
                    r0 = i * group + h * half
                    x2[g, 2 * h * half : (2 * h + 1) * half, cols] = both[r0 : r0 + half, :256]
                    x2[g, (2 * h + 1) * half : (2 * h + 2) * half, cols] = both[r0 : r0 + half, 256:]

    def partial_send(s):
        return remote(pbuf.at[s, other], prec.at[s], ps_s.at[s], ps_r.at[s], x_peer)

    def hidden_send(s):
        return remote(hid.at[s, rep], hid.at[s, rep], hs_s.at[s], hs_r.at[s], x_peer)

    def hidden_recv(s):
        return remote(hid.at[s, other], hid.at[s, other], hs_s.at[s], hs_r.at[s], x_peer)

    def finish(s):
        partial_send(s).wait_recv()
        total = pbuf[s, rep].astype(jnp.float32) + prec[s].astype(jnp.float32)
        hid[s, rep] = (jax.nn.silu(total[:half]) * total[half:]).astype(jnp.bfloat16)
        hidden_send(s).start()

    def up_chunk(g, j):
        acc = jnp.dot(x2[g], wgu[j], preferred_element_type=jnp.float32)
        pbuf[g * chunks + j] = acc.astype(jnp.bfloat16).reshape(2, 2 * half, cw)
        partial_send(g * chunks + j).start()

    for e in range(3):
        gather(0, e).start()
    to_core(0, 3).start()
    mirror().start()
    for e in (2, 0, 1):
        gather(0, e).wait_recv()
        to_core(0, e).start()
    for e in range(4):
        to_core(0, e).wait_recv()
    spread_group(0)
    mirror().wait_recv()
    for e in range(3):
        gather(1, e).start()
    to_core(1, 3).start()

    @pl.loop(0, chunks)
    def _(j):
        gu_copy(j).wait()
        up_chunk(0, j)

        @pl.when(j >= lag)
        def _():
            finish(j - lag)

    early = 2
    for j in range(early):
        finish(chunks - lag + j)
    for e in (2, 0, 1):
        gather(1, e).wait_recv()
        to_core(1, e).start()
    for e in range(4):
        to_core(1, e).wait_recv()
    spread_group(1)

    @pl.loop(0, chunks)
    def _(j):
        up_chunk(1, j)

        @pl.when(j >= early)
        def _():
            finish(chunks + j - lag)

    mark = lax.broadcasted_iota(jnp.int32, (group, 128), 1)

    def scale_of(g):
        lanes = xg[g, :, :, width : width + 128].reshape(group, 128).astype(jnp.float32)
        return jnp.sum(jnp.where(lax.rem(mark, n) == me, lanes, 0.0), axis=1, keepdims=True)

    def hidden_cols(g, j0, j1):
        return jnp.concatenate(
            [hid[g * chunks + j].reshape(group, cw) for j in range(j0, j1)], axis=1
        )

    def core_send(g, q):
        return remote(cbuf.at[g, q, 1 - c], crec.at[g, q], rc_s.at[g, q], rc_r.at[g, q], core_peer)

    def near_send(g, q, e):
        a, b = near[e]
        return remote(
            rbuf.at[g, q, a * 2 + b], rrec.at[g, q, e], rr_s.at[g, q, e], rr_r.at[g, q, e], near_peers[e]
        )

    def far_send(q):
        return remote(fbuf.at[q], frec.at[q], rf_s.at[q], rf_r.at[q], far_peer)

    def hand_out(g, q, made):
        mixed = (made.astype(jnp.bfloat16).astype(jnp.float32) * scale_of(g)).astype(jnp.bfloat16)
        mixed = mixed.reshape(8, rows, pw)
        for b in range(8):
            cbuf[g, q, b % 2, b // 2] = mixed[b]
        core_send(g, q).start()

    def produce(q):
        made = jnp.dot(
            hidden_cols(0, 0, chunks), wdn[:, q * pw : (q + 1) * pw], preferred_element_type=jnp.float32
        )
        hand_out(0, q, made)

    mid = chunks // 2

    def first_part(q):
        dacc[:, q * pw : (q + 1) * pw] = jnp.dot(
            hidden_cols(1, 0, mid), wdn[: mid * cw, q * pw : (q + 1) * pw],
            preferred_element_type=jnp.float32,
        )

    def second_part(q):
        made = dacc[:, q * pw : (q + 1) * pw] + jnp.dot(
            hidden_cols(1, mid, chunks), wdn[mid * cw :, q * pw : (q + 1) * pw],
            preferred_element_type=jnp.float32,
        )
        hand_out(1, q, made)

    def over_core(g, q):
        core_send(g, q).wait_recv()
        rbuf[g, q] = (cbuf[g, q, c].astype(jnp.float32) + crec[g, q].astype(jnp.float32)).astype(jnp.bfloat16)
        for e in range(3):
            near_send(g, q, e).start()

    def over_near(g, q):
        total = rbuf[g, q, zl * 2 + y].astype(jnp.float32)
        for e in range(3):
            near_send(g, q, e).wait_recv()
            total = total + rrec[g, q, e].astype(jnp.float32)
        if g == 0:
            oacc[q] = total
        else:
            fbuf[q] = total.astype(jnp.bfloat16)
            far_send(q).start()

    def last(q):
        far_send(q).wait_recv()
        out_ref[:, q * pw : (q + 1) * pw] = (oacc[q] + frec[q].astype(jnp.float32)).astype(jnp.bfloat16)

    rest = [2 * chunks - lag + i for i in range(lag)]
    for q in range(pieces):
        dn_copy(q).wait()
    for s in range(chunks):
        hidden_recv(s).wait_recv()
    finish(rest.pop(0))
    for q in range(pieces):
        produce(q)
        if rest:
            finish(rest.pop(0))
    for q in range(pieces):
        over_core(0, q)
        if rest:
            finish(rest.pop(0))
    while rest:
        finish(rest.pop(0))
    for s in range(chunks, chunks + mid):
        hidden_recv(s).wait_recv()
    for q in range(pieces):
        first_part(q)
    for q in range(pieces):
        over_near(0, q)
    for s in range(chunks + mid, 2 * chunks):
        hidden_recv(s).wait_recv()
    for step in range(pieces + 3):
        if step < pieces:
            second_part(step)
        if 0 <= step - 1 < pieces:
            over_core(1, step - 1)
        if 0 <= step - 2 < pieces:
            over_near(1, step - 2)
        if 0 <= step - 3 < pieces:
            last(step - 3)

    mirror().wait_send()
    for g in range(2):
        for e in range(3):
            gather(g, e).wait_send()
        for e in range(4):
            to_core(g, e).wait_send()
        for q in range(pieces):
            core_send(g, q).wait_send()
            for e in range(3):
                near_send(g, q, e).wait_send()
    for s in range(2 * chunks):
        partial_send(s).wait_send()
        hidden_send(s).wait_send()
    for q in range(pieces):
        far_send(q).wait_send()


def fused_on_device(tokens, gate_up, w_down, routes, gates):
    _, rows, width = tokens.shape
    hidden_units = w_down.shape[1]
    chunks, pieces, lag = hidden_units // 256, 2, 5
    pw, group, half = width // pieces, 8 * rows, 4 * rows
    bf16, dma = jnp.bfloat16, pltpu.SemaphoreType.DMA
    vmem = pl.BlockSpec(memory_space=pltpu.VMEM)
    anywhere = pl.BlockSpec(memory_space=pl.ANY)
    mixed_out = pl.pallas_call(
        functools.partial(fused_kernel, chunks, pieces, lag),
        out_shape=jax.ShapeDtypeStruct((rows, width), bf16),
        in_specs=[vmem, anywhere, anywhere, vmem, vmem],
        out_specs=vmem,
        scratch_shapes=[
            pltpu.VMEM((2, 8, rows, width + 128), bf16),
            pltpu.VMEM((chunks, 2 * width, 256), bf16),
            pltpu.VMEM((hidden_units, width), bf16),
            pltpu.VMEM((2, 2 * group, 2 * width), bf16),
            pltpu.VMEM((2 * chunks, 2, 2 * half, 256), bf16),
            pltpu.VMEM((2 * chunks, 2 * half, 256), bf16),
            pltpu.VMEM((2 * chunks, 2, half, 256), bf16),
            pltpu.VMEM((group, width), jnp.float32),
            pltpu.VMEM((2, pieces, 2, 4, rows, pw), bf16),
            pltpu.VMEM((2, pieces, 4, rows, pw), bf16),
            pltpu.VMEM((2, pieces, 4, rows, pw), bf16),
            pltpu.VMEM((2, pieces, 3, rows, pw), bf16),
            pltpu.VMEM((pieces, rows, pw), jnp.float32),
            pltpu.VMEM((pieces, rows, pw), bf16),
            pltpu.VMEM((pieces, rows, pw), bf16),
            dma((chunks,)), dma((pieces,)),
            dma((2, 3)), dma((2, 3)), dma(()), dma(()), dma((2, 4)), dma((2, 4)),
            dma((2 * chunks,)), dma((2 * chunks,)), dma((2 * chunks,)), dma((2 * chunks,)),
            dma((2, pieces)), dma((2, pieces)), dma((2, pieces, 3)), dma((2, pieces, 3)),
            dma((pieces,)), dma((pieces,)),
        ],
        compiler_params=pltpu.CompilerParams(
            collective_id=0, has_side_effects=True, vmem_limit_bytes=67043328
        ),
    )(tokens[0], gate_up[0], w_down[0], routes[0], gates[0])
    return mixed_out[None]


def fits(mesh):
    return mesh.shape["rep"] == 2 and mesh.shape["exp"] == 16


def solution(mesh):
    placed = (
        P(None, "exp", "rep"),
        P("exp", "rep", None, None),
        P("exp", None, "rep"),
        P(None, "exp", None),
        P(None, "exp", None),
    )
    return jax.shard_map(
        fused_on_device if fits(mesh) else on_device, mesh=mesh, in_specs=placed, out_specs=P(None, "exp", "rep"), check_vma=False
    )
```

time: 56.3 us -> 51.3 us (0.911)
  Pallas kernels: 54.7 us -> 49.6 us
    pallas_call x1, Pallas kernels: 54.7 us -> 49.6 us  [fused_on_device(): pl.pallas_call(functools.partial(fused_kernel, chunks, pieces, lag), out_...]
where the time goes in v1:
time: 51.3 us; the launch traced here: 51.1 us
  Pallas kernels  49.6 us (97%)
  local copies, waits for them, and re-layouts  1.45 us (3%)
    pallas_call x1, Pallas kernels, fused_on_device(): pl.pallas_call(functools.partial(fused_kernel, chunks, pieces, lag), out_...  49.6 us
    unnamed x1, local copies, waits for them, and re-layouts  1.45 us

profile of v1, /device:TPU:0, one launch (start us, length us, event | category | flops | bytes accessed | tf_op | source)
XLA Modules:
  0.0 51.1 jit_solution(17440340061194012569)
XLA Ops:
  0.0 49.6 %shard_map.55 = bf16[8,3584]{1,0:T(8,128)(2,1)} custom-call(bf16[8,3584]{1,0:T(8,128)(2,1)} %bitcast.9, bf16[3584,2,2048]{2,1,0:T(2,128)(2,1)} %bitcast.6, bf16[2048,3584]{1,0:T(8,128)(2,1)} %bitcast.7, s32[8,8]{1,0:T(8,128)} %bitcast.10, f32[8,8]{1,0:T(8,128)} %bitcast.11), custom_call_target="tpu_custom_call" | custom-call | tf_op jit(solution)/shard_map/pallas_call | solution.py:355
  49.6 1.4 %copy.7 = bf16[1,8,3584]{2,1,0:T(8,128)(2,1)} copy(bf16[1,8,3584]{2,1,0:T(8,128)(2,1)} %bitcast.8) | data formatting | bytes 114688

commit v2 on v1

--- a/solution.py
+++ b/solution.py
@@ -60,9 +60,9 @@
 
 
 def fused_kernel(
-    chunks, pieces, lag, tok_ref, gu_ref, dn_ref, routes_ref, gates_ref, out_ref,
+    chunks, pieces, tok_ref, gu_ref, dn_ref, routes_ref, gates_ref, out_ref,
     xg, wgu, wdn, x2, pbuf, prec, hid, dacc, cbuf, crec, rbuf, rrec, oacc, fbuf, frec,
-    gu_sem, dn_sem, ag_s, ag_r, mi_s, mi_r, dc_s, dc_r,
+    picks, shares, obuf, in_sem, out_sem, gu_sem, dn_sem, ag_s, ag_r, mi_s, mi_r, dc_s, dc_r,
     ps_s, ps_r, hs_s, hs_r, rc_s, rc_r, rr_s, rr_r, rf_s, rf_r,
 ):
     rep = lax.axis_index("rep")
@@ -104,24 +104,32 @@
             gu_rows.at[:, pl.ds(pl.multiple_of(j * cw, 128), cw)], wgu.at[j], gu_sem.at[j]
         )
 
-    def dn_copy(q):
-        cols = pl.ds(q * pw, pw)
-        return pltpu.make_async_copy(dn_ref.at[:, cols], wdn.at[:, cols], dn_sem.at[q])
-
+    mid = chunks // 2
+
+    def dn_copy(k):
+        part = pl.ds(k * mid * cw, mid * cw)
+        return pltpu.make_async_copy(dn_ref.at[part], wdn.at[part], dn_sem.at[k])
+
+    own = [
+        pltpu.make_async_copy(routes_ref, picks, in_sem.at[0]),
+        pltpu.make_async_copy(gates_ref, shares, in_sem.at[1]),
+        pltpu.make_async_copy(tok_ref, xg.at[0, at, :, pl.ds(0, width)], in_sem.at[2]),
+    ]
+    for copy in own:
+        copy.start()
     for j in range(chunks):
         gu_copy(j).start()
-    for q in range(pieces):
-        dn_copy(q).start()
-
+    own[0].wait()
+    own[1].wait()
     lane = lax.broadcasted_iota(jnp.int32, (rows, 128), 1)
     weight = jnp.zeros((rows, 128), jnp.float32)
-    for k in range(routes_ref.shape[1]):
-        hit = routes_ref[:, k : k + 1] == lax.rem(lane, n)
-        weight = weight + jnp.where(hit, gates_ref[:, k : k + 1], 0.0)
+    for k in range(picks.shape[1]):
+        hit = picks[:, k : k + 1] == lax.rem(lane, n)
+        weight = weight + jnp.where(hit, shares[:, k : k + 1], 0.0)
     high = weight.astype(jnp.bfloat16).astype(jnp.float32)
     packed = jnp.where(lane < n, high, jnp.where(lane < 2 * n, weight - high, 0.0))
-    xg[0, at, :, 0:width] = tok_ref[...]
     xg[0, at, :, width : width + 128] = packed.astype(jnp.bfloat16)
+    own[2].wait()
     pl.semaphore_wait(barrier, len(peers))
 
     def gather(g, e):
@@ -188,6 +196,8 @@
         to_core(0, e).start()
     for e in range(4):
         to_core(0, e).wait_recv()
+    for k in range(2):
+        dn_copy(k).start()
     spread_group(0)
     mirror().wait_recv()
     for e in range(3):
@@ -199,25 +209,26 @@
         gu_copy(j).wait()
         up_chunk(0, j)
 
-        @pl.when(j >= lag)
-        def _():
-            finish(j - lag)
-
     early = 2
     for j in range(early):
-        finish(chunks - lag + j)
+        finish(j)
     for e in (2, 0, 1):
         gather(1, e).wait_recv()
         to_core(1, e).start()
     for e in range(4):
         to_core(1, e).wait_recv()
     spread_group(1)
+    lag = 5
 
     @pl.loop(0, chunks)
     def _(j):
         up_chunk(1, j)
 
-        @pl.when(j >= early)
+        @pl.when(j < mid - early)
+        def _():
+            finish(early + j)
+
+        @pl.when(j >= lag)
         def _():
             finish(chunks + j - lag)
 
@@ -226,6 +237,8 @@
     def scale_of(g):
         lanes = xg[g, :, :, width : width + 128].reshape(group, 128).astype(jnp.float32)
         return jnp.sum(jnp.where(lax.rem(mark, n) == me, lanes, 0.0), axis=1, keepdims=True)
+
+    scales = [scale_of(g) for g in range(2)]
 
     def hidden_cols(g, j0, j1):
         return jnp.concatenate(
@@ -245,32 +258,24 @@
         return remote(fbuf.at[q], frec.at[q], rf_s.at[q], rf_r.at[q], far_peer)
 
     def hand_out(g, q, made):
-        mixed = (made.astype(jnp.bfloat16).astype(jnp.float32) * scale_of(g)).astype(jnp.bfloat16)
+        mixed = (made.astype(jnp.bfloat16).astype(jnp.float32) * scales[g]).astype(jnp.bfloat16)
         mixed = mixed.reshape(8, rows, pw)
         for b in range(8):
             cbuf[g, q, b % 2, b // 2] = mixed[b]
         core_send(g, q).start()
 
-    def produce(q):
-        made = jnp.dot(
-            hidden_cols(0, 0, chunks), wdn[:, q * pw : (q + 1) * pw], preferred_element_type=jnp.float32
-        )
-        hand_out(0, q, made)
-
-    mid = chunks // 2
-
-    def first_part(q):
-        dacc[:, q * pw : (q + 1) * pw] = jnp.dot(
-            hidden_cols(1, 0, mid), wdn[: mid * cw, q * pw : (q + 1) * pw],
-            preferred_element_type=jnp.float32,
-        )
-
-    def second_part(q):
-        made = dacc[:, q * pw : (q + 1) * pw] + jnp.dot(
-            hidden_cols(1, mid, chunks), wdn[mid * cw :, q * pw : (q + 1) * pw],
-            preferred_element_type=jnp.float32,
-        )
-        hand_out(1, q, made)
+    def first_part(g, q):
+        cols = slice(q * pw, (q + 1) * pw)
+        dacc[g, :, cols] = jnp.dot(
+            hidden_cols(g, 0, mid), wdn[: mid * cw, cols], preferred_element_type=jnp.float32
+        )
+
+    def second_part(g, q):
+        cols = slice(q * pw, (q + 1) * pw)
+        made = dacc[g, :, cols] + jnp.dot(
+            hidden_cols(g, mid, chunks), wdn[mid * cw :, cols], preferred_element_type=jnp.float32
+        )
+        hand_out(g, q, made)
 
     def over_core(g, q):
         core_send(g, q).wait_recv()
@@ -289,43 +294,60 @@
             fbuf[q] = total.astype(jnp.bfloat16)
             far_send(q).start()
 
+    def put(q):
+        cols = pl.ds(q * pw, pw)
+        return pltpu.make_async_copy(obuf.at[:, cols], out_ref.at[:, cols], out_sem.at[q])
+
     def last(q):
         far_send(q).wait_recv()
-        out_ref[:, q * pw : (q + 1) * pw] = (oacc[q] + frec[q].astype(jnp.float32)).astype(jnp.bfloat16)
-
-    rest = [2 * chunks - lag + i for i in range(lag)]
-    for q in range(pieces):
-        dn_copy(q).wait()
-    for s in range(chunks):
+        obuf[:, q * pw : (q + 1) * pw] = (oacc[q] + frec[q].astype(jnp.float32)).astype(jnp.bfloat16)
+        put(q).start()
+
+    for k in range(2):
+        dn_copy(k).wait()
+    for s in range(mid):
         hidden_recv(s).wait_recv()
-    finish(rest.pop(0))
-    for q in range(pieces):
-        produce(q)
-        if rest:
-            finish(rest.pop(0))
-    for q in range(pieces):
-        over_core(0, q)
-        if rest:
-            finish(rest.pop(0))
-    while rest:
-        finish(rest.pop(0))
+    late = [2 * chunks - lag + i for i in range(lag)]
+    spare = list(range(mid, chunks))
+    for q in range(pieces):
+        first_part(0, q)
+        if q % 2 == 1 and late:
+            finish(late.pop(0))
+            if spare:
+                finish(spare.pop(0))
+    while late:
+        if spare:
+            finish(spare.pop(0))
+        finish(late.pop(0))
+    while spare:
+        finish(spare.pop(0))
     for s in range(chunks, chunks + mid):
         hidden_recv(s).wait_recv()
     for q in range(pieces):
-        first_part(q)
-    for q in range(pieces):
-        over_near(0, q)
+        first_part(1, q)
     for s in range(chunks + mid, 2 * chunks):
         hidden_recv(s).wait_recv()
-    for step in range(pieces + 3):
-        if step < pieces:
-            second_part(step)
-        if 0 <= step - 1 < pieces:
-            over_core(1, step - 1)
-        if 0 <= step - 2 < pieces:
-            over_near(1, step - 2)
-        if 0 <= step - 3 < pieces:
-            last(step - 3)
+    behind = 4
+    for q in range(pieces):
+        second_part(1, q)
+        if q >= behind:
+            over_core(1, q - behind)
+    for s in range(mid, chunks):
+        hidden_recv(s).wait_recv()
+    for q in range(pieces):
+        second_part(0, q)
+        if pieces - behind + q < pieces:
+            over_core(1, pieces - behind + q)
+        if q >= behind:
+            over_core(0, q - behind)
+    for q in range(pieces - behind, pieces):
+        over_core(0, q)
+    for q in range(pieces):
+        over_near(1, q)
+    for q in range(pieces):
+        over_near(0, q)
+    for q in range(pieces):
+        last(q)
 
     mirror().wait_send()
     for g in range(2):
@@ -342,21 +364,21 @@
         hidden_send(s).wait_send()
     for q in range(pieces):
         far_send(q).wait_send()
+        put(q).wait()
 
 
 def fused_on_device(tokens, gate_up, w_down, routes, gates):
     _, rows, width = tokens.shape
     hidden_units = w_down.shape[1]
-    chunks, pieces, lag = hidden_units // 256, 2, 5
+    chunks, pieces = hidden_units // 256, width // 512
     pw, group, half = width // pieces, 8 * rows, 4 * rows
     bf16, dma = jnp.bfloat16, pltpu.SemaphoreType.DMA
-    vmem = pl.BlockSpec(memory_space=pltpu.VMEM)
     anywhere = pl.BlockSpec(memory_space=pl.ANY)
     mixed_out = pl.pallas_call(
-        functools.partial(fused_kernel, chunks, pieces, lag),
+        functools.partial(fused_kernel, chunks, pieces),
         out_shape=jax.ShapeDtypeStruct((rows, width), bf16),
-        in_specs=[vmem, anywhere, anywhere, vmem, vmem],
-        out_specs=vmem,
+        in_specs=[anywhere] * 5,
+        out_specs=anywhere,
         scratch_shapes=[
             pltpu.VMEM((2, 8, rows, width + 128), bf16),
             pltpu.VMEM((chunks, 2 * width, 256), bf16),
@@ -365,7 +387,7 @@
             pltpu.VMEM((2 * chunks, 2, 2 * half, 256), bf16),
             pltpu.VMEM((2 * chunks, 2 * half, 256), bf16),
             pltpu.VMEM((2 * chunks, 2, half, 256), bf16),
-            pltpu.VMEM((group, width), jnp.float32),
+            pltpu.VMEM((2, group, width), jnp.float32),
             pltpu.VMEM((2, pieces, 2, 4, rows, pw), bf16),
             pltpu.VMEM((2, pieces, 4, rows, pw), bf16),
             pltpu.VMEM((2, pieces, 4, rows, pw), bf16),
@@ -373,7 +395,10 @@
             pltpu.VMEM((pieces, rows, pw), jnp.float32),
             pltpu.VMEM((pieces, rows, pw), bf16),
             pltpu.VMEM((pieces, rows, pw), bf16),
-            dma((chunks,)), dma((pieces,)),
+            pltpu.VMEM(routes.shape[1:], routes.dtype),
+            pltpu.VMEM(gates.shape[1:], gates.dtype),
+            pltpu.VMEM((rows, width), bf16),
+            dma((3,)), dma((pieces,)), dma((chunks,)), dma((2,)),
             dma((2, 3)), dma((2, 3)), dma(()), dma(()), dma((2, 4)), dma((2, 4)),
             dma((2 * chunks,)), dma((2 * chunks,)), dma((2 * chunks,)), dma((2 * chunks,)),
             dma((2, pieces)), dma((2, pieces)), dma((2, pieces, 3)), dma((2, pieces, 3)),

time: 51.3 us -> 48.5 us (0.945)
  Pallas kernels: 49.6 us -> 46.9 us
    pallas_call x1, Pallas kernels: 49.6 us -> 46.9 us  [fused_on_device(): pl.pallas_call(functools.partial(fused_kernel, chunks, pieces), out_shape...]
where the time goes in v2:
time: 48.5 us; the launch traced here: 48.4 us
  Pallas kernels  46.9 us (97%)
  local copies, waits for them, and re-layouts  1.45 us (3%)
    pallas_call x1, Pallas kernels, fused_on_device(): pl.pallas_call(functools.partial(fused_kernel, chunks, pieces), out_shape...  46.9 us
    unnamed x1, local copies, waits for them, and re-layouts  1.45 us

profile of v2, /device:TPU:0, one launch (start us, length us, event | category | flops | bytes accessed | tf_op | source)
XLA Modules:
  0.0 48.4 jit_solution(8632298782986467038)
XLA Ops:
  0.0 46.9 %shard_map.55 = bf16[8,3584]{1,0:T(8,128)(2,1)} custom-call(bf16[8,3584]{1,0:T(8,128)(2,1)} %bitcast.9, bf16[3584,2,2048]{2,1,0:T(2,128)(2,1)} %bitcast.6, bf16[2048,3584]{1,0:T(8,128)(2,1)} %bitcast.7, s32[8,8]{1,0:T(8,128)} %bitcast.10, f32[8,8]{1,0:T(8,128)} %bitcast.11), custom_call_target="tpu_custom_call" | custom-call | tf_op jit(solution)/shard_map/pallas_call | solution.py:377
  46.9 1.4 %copy.7 = bf16[1,8,3584]{2,1,0:T(8,128)(2,1)} copy(bf16[1,8,3584]{2,1,0:T(8,128)(2,1)} %bitcast.8) | data formatting | bytes 114688

commit v3 on v2

--- a/solution.py
+++ b/solution.py
@@ -60,9 +60,9 @@
 
 
 def fused_kernel(
-    chunks, pieces, tok_ref, gu_ref, dn_ref, routes_ref, gates_ref, out_ref,
-    xg, wgu, wdn, x2, pbuf, prec, hid, dacc, cbuf, crec, rbuf, rrec, oacc, fbuf, frec,
-    picks, shares, obuf, in_sem, out_sem, gu_sem, dn_sem, ag_s, ag_r, mi_s, mi_r, dc_s, dc_r,
+    chunks, pieces, tok_ref, gu_ref, dn_ref, routes_ref, gates_ref, near_ref, far_ref,
+    xg, wgu, wdn, x2, pbuf, prec, hid, dacc, cbuf, crec, rbuf, rrec, oacc, fbuf,
+    picks, shares, in_sem, out_sem, gu_sem, dn_sem, ag_s, ag_r, mi_s, mi_r, dc_s, dc_r,
     ps_s, ps_r, hs_s, hs_r, rc_s, rc_r, rr_s, rr_r, rf_s, rf_r,
 ):
     rep = lax.axis_index("rep")
@@ -144,17 +144,17 @@
         slot = xg.at[g, a * 4 + b * 2 + c]
         return remote(slot, slot, dc_s.at[g, e], dc_r.at[g, e], core_peer)
 
-    def spread_group(g):
+    def spread_half(g, h):
         row_at = lax.broadcasted_iota(jnp.int32, (128, 512), 0)
         col_at = lax.broadcasted_iota(jnp.int32, (128, 512), 1)
         target = jnp.where(col_at < 256, 2 * row_at, 256 + 2 * row_at + 1)
         spread = jnp.where(col_at == target, 1.0, 0.0).astype(jnp.bfloat16)
-        batch = 7
+        batch = 14
 
         @pl.loop(0, width // (128 * batch))
         def _(t):
             parts = [
-                xg[g, :, :, pl.ds(pl.multiple_of((t * batch + i) * 128, 128), 128)].reshape(group, 128)
+                xg[g, pl.ds(h * 4, 4), :, pl.ds(pl.multiple_of((t * batch + i) * 128, 128), 128)].reshape(half, 128)
                 for i in range(batch)
             ]
             both = jnp.dot(
@@ -162,10 +162,8 @@
             ).astype(jnp.bfloat16)
             for i in range(batch):
                 cols = pl.ds(pl.multiple_of((t * batch + i) * 256, 256), 256)
-                for h in range(2):
-                    r0 = i * group + h * half
-                    x2[g, 2 * h * half : (2 * h + 1) * half, cols] = both[r0 : r0 + half, :256]
-                    x2[g, (2 * h + 1) * half : (2 * h + 2) * half, cols] = both[r0 : r0 + half, 256:]
+                x2[g, h, :half, cols] = both[i * half : (i + 1) * half, :256]
+                x2[g, h, half:, cols] = both[i * half : (i + 1) * half, 256:]
 
     def partial_send(s):
         return remote(pbuf.at[s, other], prec.at[s], ps_s.at[s], ps_r.at[s], x_peer)
@@ -183,7 +181,7 @@
         hidden_send(s).start()
 
     def up_chunk(g, j):
-        acc = jnp.dot(x2[g], wgu[j], preferred_element_type=jnp.float32)
+        acc = jnp.dot(x2[g].reshape(2 * group, 2 * width), wgu[j], preferred_element_type=jnp.float32)
         pbuf[g * chunks + j] = acc.astype(jnp.bfloat16).reshape(2, 2 * half, cw)
         partial_send(g * chunks + j).start()
 
@@ -191,14 +189,19 @@
         gather(0, e).start()
     to_core(0, 3).start()
     mirror().start()
-    for e in (2, 0, 1):
+    for e in (2, 0):
         gather(0, e).wait_recv()
         to_core(0, e).start()
-    for e in range(4):
+    for e in (3, 2):
         to_core(0, e).wait_recv()
+    spread_half(0, zl)
+    gather(0, 1).wait_recv()
+    to_core(0, 1).start()
     for k in range(2):
         dn_copy(k).start()
-    spread_group(0)
+    for e in range(2):
+        to_core(0, e).wait_recv()
+    spread_half(0, 1 - zl)
     mirror().wait_recv()
     for e in range(3):
         gather(1, e).start()
@@ -217,7 +220,8 @@
         to_core(1, e).start()
     for e in range(4):
         to_core(1, e).wait_recv()
-    spread_group(1)
+    for h in range(2):
+        spread_half(1, h)
     lag = 5
 
     @pl.loop(0, chunks)
@@ -255,7 +259,8 @@
         )
 
     def far_send(q):
-        return remote(fbuf.at[q], frec.at[q], rf_s.at[q], rf_r.at[q], far_peer)
+        cols = pl.ds(q * pw, pw)
+        return remote(fbuf.at[q], far_ref.at[:, cols], rf_s.at[q], rf_r.at[q], far_peer)
 
     def hand_out(g, q, made):
         mixed = (made.astype(jnp.bfloat16).astype(jnp.float32) * scales[g]).astype(jnp.bfloat16)
@@ -290,18 +295,13 @@
             total = total + rrec[g, q, e].astype(jnp.float32)
         if g == 0:
             oacc[q] = total
+            put(q).start()
         else:
             fbuf[q] = total.astype(jnp.bfloat16)
             far_send(q).start()
 
     def put(q):
-        cols = pl.ds(q * pw, pw)
-        return pltpu.make_async_copy(obuf.at[:, cols], out_ref.at[:, cols], out_sem.at[q])
-
-    def last(q):
-        far_send(q).wait_recv()
-        obuf[:, q * pw : (q + 1) * pw] = (oacc[q] + frec[q].astype(jnp.float32)).astype(jnp.bfloat16)
-        put(q).start()
+        return pltpu.make_async_copy(oacc.at[q], near_ref.at[:, pl.ds(q * pw, pw)], out_sem.at[q])
 
     for k in range(2):
         dn_copy(k).wait()
@@ -347,7 +347,7 @@
     for q in range(pieces):
         over_near(0, q)
     for q in range(pieces):
-        last(q)
+        far_send(q).wait_recv()
 
     mirror().wait_send()
     for g in range(2):
@@ -374,16 +374,19 @@
     pw, group, half = width // pieces, 8 * rows, 4 * rows
     bf16, dma = jnp.bfloat16, pltpu.SemaphoreType.DMA
     anywhere = pl.BlockSpec(memory_space=pl.ANY)
-    mixed_out = pl.pallas_call(
+    near_sum, far_sum = pl.pallas_call(
         functools.partial(fused_kernel, chunks, pieces),
-        out_shape=jax.ShapeDtypeStruct((rows, width), bf16),
+        out_shape=[
+            jax.ShapeDtypeStruct((rows, width), jnp.float32),
+            jax.ShapeDtypeStruct((rows, width), bf16),
+        ],
         in_specs=[anywhere] * 5,
-        out_specs=anywhere,
+        out_specs=[anywhere] * 2,
         scratch_shapes=[
             pltpu.VMEM((2, 8, rows, width + 128), bf16),
             pltpu.VMEM((chunks, 2 * width, 256), bf16),
             pltpu.VMEM((hidden_units, width), bf16),
-            pltpu.VMEM((2, 2 * group, 2 * width), bf16),
+            pltpu.VMEM((2, 2, group, 2 * width), bf16),
             pltpu.VMEM((2 * chunks, 2, 2 * half, 256), bf16),
             pltpu.VMEM((2 * chunks, 2 * half, 256), bf16),
             pltpu.VMEM((2 * chunks, 2, half, 256), bf16),
@@ -394,10 +397,8 @@
             pltpu.VMEM((2, pieces, 3, rows, pw), bf16),
             pltpu.VMEM((pieces, rows, pw), jnp.float32),
             pltpu.VMEM((pieces, rows, pw), bf16),
-            pltpu.VMEM((pieces, rows, pw), bf16),
             pltpu.VMEM(routes.shape[1:], routes.dtype),
             pltpu.VMEM(gates.shape[1:], gates.dtype),
-            pltpu.VMEM((rows, width), bf16),
             dma((3,)), dma((pieces,)), dma((chunks,)), dma((2,)),
             dma((2, 3)), dma((2, 3)), dma(()), dma(()), dma((2, 4)), dma((2, 4)),
             dma((2 * chunks,)), dma((2 * chunks,)), dma((2 * chunks,)), dma((2 * chunks,)),
@@ -408,7 +409,7 @@
             collective_id=0, has_side_effects=True, vmem_limit_bytes=67043328
         ),
     )(tokens[0], gate_up[0], w_down[0], routes[0], gates[0])
-    return mixed_out[None]
+    return (near_sum + far_sum.astype(jnp.float32)).astype(bf16)[None]
 
 
 def fits(mesh):

time: 48.5 us -> 47.7 us (0.984)
  other arithmetic: 0 us -> 1.54 us
  local copies, waits for them, and re-layouts: 1.45 us -> 0 us
  Pallas kernels: 46.9 us -> 46 us
    broadcast_in_dim x0 -> x1, other arithmetic: none -> 1.54 us  [fused_on_device(): return (near_sum + far_sum.astype(jnp.float32)).astype(bf16)[None]]
    unnamed x1 -> x0, local copies, waits for them, and re-layouts: 1.45 us -> none
    pallas_call x1, Pallas kernels: 46.9 us -> 46 us  [fused_on_device(): pl.pallas_call(functools.partial(fused_kernel, chunks, pieces), out_shape...]
where the time goes in v3:
time: 47.7 us; the launch traced here: 47.6 us
  Pallas kernels  46 us (96%)
  other arithmetic  1.54 us (3%)
    pallas_call x1, Pallas kernels, fused_on_device(): pl.pallas_call(functools.partial(fused_kernel, chunks, pieces), out_shape...  46 us
    broadcast_in_dim x1, other arithmetic, fused_on_device(): return (near_sum + far_sum.astype(jnp.float32)).astype(bf16)[None]  1.54 us

profile of v3, /device:TPU:0, one launch (start us, length us, event | category | flops | bytes accessed | tf_op | source)
XLA Modules:
  0.0 47.6 jit_solution(9983462243739483353)
XLA Ops:
  0.0 46.0 %shard_map.55 = (f32[8,3584]{1,0:T(8,128)}, bf16[8,3584]{1,0:T(8,128)(2,1)}) custom-call(bf16[8,3584]{1,0:T(8,128)(2,1)} %bitcast.9, bf16[3584,2,2048]{2,1,0:T(2,128)(2,1)} %bitcast.7, bf16[2048,3584]{1,0:T(8,128)(2,1)} %bitcast.8, s32[8,8]{1,0:T(8,128)} %bitcast.10, f32[8,8]{1,0:T(8,128)} %bitcast.11), custom_call_target="tpu_custom_call" | custom-call | tf_op jit(solution)/shard_map/pallas_call | solution.py:377
  46.0 1.5 %fusion = bf16[1,8,3584]{2,1,0:T(8,128)(2,1)} fusion(f32[8,3584]{1,0:T(8,128)} %get-tuple-element.7, bf16[8,3584]{1,0:T(8,128)(2,1)} %get-tuple-element.8), kind=kLoop, calls=%fused_computation.1 | loop fusion | flops 86016 | bytes 229376 | tf_op jit(solution)/shard_map/broadcast_in_dim | solution.py:412

commit v4 on v3

--- a/solution.py
+++ b/solution.py
@@ -185,7 +185,7 @@
         pbuf[g * chunks + j] = acc.astype(jnp.bfloat16).reshape(2, 2 * half, cw)
         partial_send(g * chunks + j).start()
 
-    for e in range(3):
+    for e in (1, 2, 0):
         gather(0, e).start()
     to_core(0, 3).start()
     mirror().start()
@@ -203,7 +203,7 @@
         to_core(0, e).wait_recv()
     spread_half(0, 1 - zl)
     mirror().wait_recv()
-    for e in range(3):
+    for e in (1, 2, 0):
         gather(1, e).start()
     to_core(1, 3).start()
 
@@ -285,7 +285,7 @@
     def over_core(g, q):
         core_send(g, q).wait_recv()
         rbuf[g, q] = (cbuf[g, q, c].astype(jnp.float32) + crec[g, q].astype(jnp.float32)).astype(jnp.bfloat16)
-        for e in range(3):
+        for e in (1, 2, 0):
             near_send(g, q, e).start()
 
     def over_near(g, q):

time: 47.7 us -> 47.2 us (0.990)
  Pallas kernels: 46 us -> 45.4 us
    pallas_call x1, Pallas kernels: 46 us -> 45.4 us  [fused_on_device(): pl.pallas_call(functools.partial(fused_kernel, chunks, pieces), out_shape...]
where the time goes in v4:
time: 47.2 us; the launch traced here: 47 us
  Pallas kernels  45.4 us (96%)
  other arithmetic  1.54 us (3%)
    pallas_call x1, Pallas kernels, fused_on_device(): pl.pallas_call(functools.partial(fused_kernel, chunks, pieces), out_shape...  45.4 us
    broadcast_in_dim x1, other arithmetic, fused_on_device(): return (near_sum + far_sum.astype(jnp.float32)).astype(bf16)[None]  1.54 us

profile of v4, /device:TPU:0, one launch (start us, length us, event | category | flops | bytes accessed | tf_op | source)
XLA Modules:
  0.0 47.0 jit_solution(3703646439748068227)
XLA Ops:
  0.0 45.4 %shard_map.55 = (f32[8,3584]{1,0:T(8,128)}, bf16[8,3584]{1,0:T(8,128)(2,1)}) custom-call(bf16[8,3584]{1,0:T(8,128)(2,1)} %bitcast.9, bf16[3584,2,2048]{2,1,0:T(2,128)(2,1)} %bitcast.7, bf16[2048,3584]{1,0:T(8,128)(2,1)} %bitcast.8, s32[8,8]{1,0:T(8,128)} %bitcast.10, f32[8,8]{1,0:T(8,128)} %bitcast.11), custom_call_target="tpu_custom_call" | custom-call | tf_op jit(solution)/shard_map/pallas_call | solution.py:377
  45.4 1.5 %fusion = bf16[1,8,3584]{2,1,0:T(8,128)(2,1)} fusion(f32[8,3584]{1,0:T(8,128)} %get-tuple-element.7, bf16[8,3584]{1,0:T(8,128)(2,1)} %get-tuple-element.8), kind=kLoop, calls=%fused_computation.1 | loop fusion | flops 86016 | bytes 229376 | tf_op jit(solution)/shard_map/broadcast_in_dim | solution.py:412
